TPU v7x, 256 devices: a whole 4x4x8 slice. The times are simulated.
256 devices in a mesh: dp: 32 (over x, z_lo, core), mp: 8 (over y, z_hi).
Axes of the slice: x: 4, y: 4, z: 8 (z_hi: 2, z_lo: 4; z = z_hi * 4 + z_lo), core: 2. Of those that a mesh axis runs over, the one named last changes fastest.
Arguments:
- tokens: bfloat16 [32, 1024, 3584], P('dp'), may hold values from -14 to 14
- modality: int32 [32, 8], P('dp'), may hold values from 0 to 1, as said below
- block_mask: int32 [32, 8, 8], P('dp'), may hold values from 0 to 2, as said below
- q_weight: bfloat16 [2, 3584, 2048], P(None, 'dp', 'mp'), may hold values from -0.09375 to 0.09375
- kv_weight: bfloat16 [2, 3584, 1024], P(None, 'dp'), may hold values from -0.09375 to 0.09375
- o_weight: bfloat16 [2, 2048, 3584], P(None, 'mp', 'dp'), may hold values from -0.125 to 0.125
Outputs:
- attn_out: bfloat16 [32, 1024, 3584], P('dp', 'mp')
Inputs may be any that keep to these rules, and one draw needn't show every extreme that they name: modality[s, b] names the section (0 text, 1 image) whose weights serve the 128 tokens of block b of sequence s. block_mask[s, i, j] tells which tokens of block i see block j: 0 none, 1 all, 2 those at or before the query's position; every diagonal entry is 1 or 2, every entry off the diagonal is 0 or 1.
All inputs are finite; a program needn't handle non-finite values.
Results may differ from a plain program's by a relative error of at most 0.015.
Values may be sent and summed in bfloat16 or wider, within the bound.
No kernel may reach another device: no remote copies, remote signals or barrier semaphores. Data moves between devices by JAX's collectives and lax.ppermute only.
A program may use at most 128 MiB of HBM per device.

v0:
```python
import jax
import jax.numpy as jnp
from jax import lax
from jax.sharding import PartitionSpec as P

HD = 128
KVH = 4
QHEADS = 16
BLK = 128


rope_theta = 1000000.0


def rotary_tables(length, head_width):
    half_width = head_width // 2
    frequency = rope_theta ** (-jnp.arange(half_width, dtype=jnp.float32) * 2.0 / head_width)
    angles = jnp.arange(length, dtype=jnp.float32)[:, None] * frequency[None, :]
    angles = jnp.concatenate([angles, angles], axis=1)
    return (jnp.cos(angles), jnp.sin(angles))


def rotate(values, cosine_table, sine_table):
    half_width = values.shape[-1] // 2
    turned = jnp.concatenate([-values[..., half_width:], values[..., :half_width]], axis=-1)
    return values * cosine_table[:, None, :] + turned * sine_table[:, None, :]


def project_rows(blocks, block_kinds, pieces):

    def project_one_block(inputs):
        row_block, block_kind = inputs
        return tuple(
            (
                jnp.dot(
                    row_block,
                    lax.dynamic_index_in_dim(shard_piece, block_kind, 0, keepdims=False),
                    preferred_element_type=jnp.float32,
                )
                for shard_piece in pieces
            )
        )

    products = lax.map(project_one_block, (blocks, block_kinds))
    return tuple((product for product in products))


def local(tokens, modality, block_mask, q_weight, kv_weight, o_weight):
    states = tokens[0]
    block_kinds = modality[0]
    layout = block_mask[0]
    length = states.shape[0]
    model_width = states.shape[1]
    block_count = length // BLK
    blocks = states.reshape(block_count, BLK, model_width)
    head_cols = q_weight.shape[2]
    local_heads = head_cols // HD
    group_size = QHEADS // KVH
    pair_heads = max(1, local_heads // group_size)
    pair_cols = pair_heads * 2 * HD
    model_index = lax.axis_index("mp")
    first_pair = model_index * local_heads // group_size
    kv_needed = lax.dynamic_slice_in_dim(kv_weight, first_pair * (2 * HD), pair_cols, 2)
    query_sum, pair_sum = project_rows(
        blocks,
        block_kinds,
        (
            lax.all_gather(q_weight, "dp", axis=1, tiled=True),
            lax.all_gather(kv_needed, "dp", axis=1, tiled=True),
        ),
    )
    cosine_table, sine_table = rotary_tables(length, HD)
    queries = rotate(query_sum.reshape(length, local_heads, HD), cosine_table, sine_table).astype(
        jnp.bfloat16
    )
    pair_raw = pair_sum.reshape(length, pair_heads, 2, HD)
    key_heads = rotate(pair_raw[:, :, 0], cosine_table, sine_table).astype(jnp.bfloat16)
    value_heads = pair_raw[:, :, 1].astype(jnp.bfloat16)
    queries = queries.reshape(length, pair_heads, local_heads // pair_heads, HD)
    block_rows = min(512, length)
    score_scale = HD ** (-0.5)
    positions = jnp.arange(length, dtype=jnp.int32)

    def attend(block_index):
        first_row = block_index * block_rows
        query_part = lax.dynamic_slice_in_dim(queries, first_row, block_rows, 0)
        rows_mask = lax.dynamic_slice_in_dim(layout, first_row // BLK, block_rows // BLK, 0)
        expanded = jnp.broadcast_to(
            rows_mask[:, None, :, None], (block_rows // BLK, BLK, block_count, BLK)
        ).reshape(block_rows, length)
        query_pos = first_row + jnp.arange(block_rows, dtype=jnp.int32)
        allowed = (expanded == 1) | (expanded == 2) & (positions[None, :] <= query_pos[:, None])
        scores = (
            jnp.einsum("qgjd,kgd->gjqk", query_part, key_heads, preferred_element_type=jnp.float32)
            * score_scale
        )
        scores = jnp.where(allowed[None, None], scores, -1e30)
        row_max = jnp.max(scores, axis=-1, keepdims=True)
        weights = jnp.exp(scores - row_max)
        weights = (weights / jnp.sum(weights, axis=-1, keepdims=True)).astype(jnp.bfloat16)
        mixed_out = jnp.einsum(
            "gjqk,kgd->qgjd", weights, value_heads, preferred_element_type=jnp.float32
        )
        return mixed_out.astype(jnp.bfloat16).reshape(block_rows, head_cols)

    attended_flat = lax.map(attend, jnp.arange(length // block_rows, dtype=jnp.int32)).reshape(
        length, head_cols
    )
    attended = attended_flat.reshape(block_count, BLK, head_cols)
    shard_piece = lax.all_gather(o_weight, "dp", axis=2, tiled=True)

    def body_one_block(inputs):
        row_block, block_kind = inputs
        chosen = lax.dynamic_index_in_dim(shard_piece, block_kind, 0, keepdims=False)
        return jnp.dot(row_block, chosen, preferred_element_type=jnp.float32)

    partial_out = lax.map(body_one_block, (attended, block_kinds))
    head_terms = partial_out.reshape(length, shard_piece.shape[2])
    summed = lax.psum_scatter(
        head_terms.astype(jnp.bfloat16), "mp", scatter_dimension=0, tiled=True
    )
    return summed[None]


def solution(mesh):
    in_specs = (
        P("dp", None, None),
        P("dp", None),
        P("dp", None, None),
        P(None, "dp", "mp"),
        P(None, "dp", None),
        P(None, "mp", "dp"),
    )
    out_specs = P("dp", "mp", None)
    return jax.shard_map(local, mesh=mesh, in_specs=in_specs, out_specs=out_specs, check_vma=False)
```

profile of v0, /device:TPU:32, one launch (start us, length us, event | category | flops | bytes accessed | tf_op | source)
XLA Modules:
  0.0 469.1 jit_solution(1920752363495440663)
XLA Ops:
  8.3 1.6 copy.25
  10.1 2.6 fusion.52
  12.7 60.4 %all-gather.4.cloned.1.call-done = bf16[2,3584,256]{2,1,0:T(8,128)(2,1)} async-done(((bf16[2,112,256]{2,1,0:T(8,128)(2,1)}), bf16[2,3584,256]{2,1,0:T(8,128)(2,1)}) %all-gather.4.cloned.1.call-update) | async-done | bytes 3670032 | tf_op jit(solution)/shard_map/all_gather | solution.py:68
  73.1 62.5 %all-gather.6.cloned.1.call-done = bf16[2,3584,256]{2,1,0:T(8,128)(2,1)} async-done(((bf16[2,112,256]{2,1,0:T(8,128)(2,1)}), bf16[2,3584,256]{2,1,0:T(8,128)(2,1)}) %all-gather.6.cloned.1.call-update) | async-done | bytes 3670032 | tf_op jit(solution)/shard_map/all_gather | solution.py:69
  135.7 63.6 %while.35 = (s32[]{:T(128)}, f32[8,128,256]{2,1,0:T(8,128)S(1)}, f32[8,128,256]{2,1,0:T(8,128)}, bf16[8,128,3584]{2,1,0:T(8,128)(2,1)}, s32[8]{0:T(128)}, /*inde...) while((s32[]{:T(128)}, f32[8,128,256]{2,1,0:T(8,128)S(1)}, ...), condition=%wide.region_1.2_spmd, body=%wide.region_0.1_spmd.sunk | while | flops 469762048 | bytes 5770395 | solution.py:44
  138.5 2.9 fusion.81
  141.4 2.2 fusion.80
  146.4 2.9 fusion.81
  149.3 2.2 fusion.80
  154.4 2.9 fusion.81
  157.2 2.2 fusion.80
  159.4 1.2 dynamic_slice.108
  162.3 2.9 fusion.81
  165.2 2.2 fusion.80
  170.3 2.9 fusion.81
  173.2 2.2 fusion.80
  178.2 2.9 fusion.81
  181.1 2.2 fusion.80
  186.3 2.8 fusion.81
  189.1 2.2 fusion.80
  194.2 2.9 fusion.81
  197.0 2.2 fusion.80
  199.2 1.7 reshape.334
  202.2 1.4 slice.30
  203.5 1.5 reshape.332
  205.6 1.9 copy.36
  207.4 1.2 copy.35
  208.7 2.0 fusion.57
  211.5 1.5 copy.27
  213.0 2.5 fusion.60
  215.5 2.2 copy.33
  217.8 1.4 copy.34
  221.4 16.6 %while.37 = (s32[]{:T(128)}, bf16[2,512,256]{2,1,0:T(8,128)(2,1)}, s32[2]{0:T(128)S(1)}, s32[8,8]{1,0:T(8,128)S(1)}, bf16[1024,1,2,128]{0,3,2,1:T(8,128)(2,1)}, ...) while((s32[]{:T(128)}, bf16[2,512,256]{2,1,0:T(8,128)(2,1)}, ...), condition=%wide.region_5.6_spmd.clone, body=%wide.region_2.5_spmd.clone.sunk | while | flops 551156352 | bytes 23093956 | solution.py:106
  223.7 2.2 fusion.88
  227.1 1.6 fusion.90
  232.0 2.2 fusion.88
  235.4 1.6 fusion.90
  238.0 10.0 %copy.26 = bf16[2,256,3584]{2,1,0:T(8,128)(2,1)} copy(bf16[2,256,3584]{1,0,2:T(2,128)(2,1)} %all-gather.8.cloned.1.call-done) | data formatting | bytes 7340032 | tf_op jit(solution)/shard_map/while | solution.py:117
  248.0 43.2 %while.36 = (s32[]{:T(128)}, bf16[8,128,3584]{2,1,0:T(8,128)(2,1)}, bf16[8,128,256]{2,1,0:T(8,128)(2,1)}, s32[8]{0:T(128)S(1)}, bf16[2,256,3584]{2,1,0:T(8,128)(2,1)}, /*index=5*/s32[]{:T(128)}, s32[]{:T(128)}, s32[]{:T(128)}) while((s32[]{:T(128)}, bf16[8,128,3584]{2,1,0:T(8,128)(2,1)}, bf16[8,128,256]{2,1,0:T(8,128)(2,1)}, s32[8]{0:T(128)S(1)}, ...), condition=%wide.region_7.8_spmd, body=%wide.region_6.7_spmd.sunk | while | flops 234881024 | bytes 3737227 | solution.py:117
  250.5 2.9 fusion.84
  255.9 2.9 fusion.84
  261.4 2.9 fusion.84
  266.8 2.9 fusion.84
  272.1 2.9 fusion.84
  277.5 2.9 fusion.84
  283.0 2.9 fusion.84
  288.4 2.9 fusion.84
  291.3 171.3 %reduce-scatter.2.cloned.1.call-done = bf16[128,3584]{1,0:T(8,128)(2,1)} async-done(((bf16[1024,3584]{1,0:T(8,128)(2,1)}), bf16[128,3584]{1,0:T(8,128)(2,1)}) %reduce-scatter.2.cloned.1.call-update) | async-done | bytes 917520 | tf_op jit(solution)/shard_map/reduce_scatter | solution.py:119
  (74 shorter events, 27.9 us)
Async XLA Ops:
  6.5 1.0 copy-start
  6.5 66.6 %all-gather.4.cloned.1.call-start = ((), (), s32[]{:S(2)}) async-start(), calls=%async_computation.1 | async-start | bytes 3784704 | tf_op jit(solution)/shard_map/all_gather | solution.py:68
  7.3 128.4 %all-gather.6.cloned.1.call-start = ((), (), s32[]{:S(2)}) async-start(), calls=%async_computation.2 | async-start | bytes 3784704 | tf_op jit(solution)/shard_map/all_gather | solution.py:69
  8.2 229.8 %all-gather.8.cloned.1.call-start = ((), (), s32[]{:S(2)}) async-start(), calls=%async_computation.3 | async-start | bytes 3784704 | tf_op jit(solution)/shard_map/all_gather | solution.py:110
  9.9 452.6 %reduce-scatter.2.cloned.1.call-start = ((), (), s32[]{:S(2)}) async-start(), calls=%async_computation.4 | async-start | bytes 8257536 | tf_op jit(solution)/shard_map/reduce_scatter | solution.py:119
  215.5 4.8 %copy-start.1 = (f32[1024,128]{0,1:T(8,128)S(1)}, f32[1024,128]{0,1:T(8,128)}, u32[]{:S(2)}) copy-start(f32[1024,128]{0,1:T(8,128)} %get-tuple-element.265) | copy-start | bytes 1572868
  215.5 5.9 %copy-start.2 = (bf16[1024,1,1,128]{0,3,2,1:T(8,128)(2,1)S(1)}, bf16[1024,1,1,128]{0,3,2,1:T(8,128)(2,1)}, u32[]{:S(2)}) copy-start(bf16[1024,1,1,128]{0,3,2,1:T(8,128)(2,1)} %copy.36) | copy-start | bytes 786436
  215.5 5.9 %copy-start.5 = (s32[1,8,8]{2,1,0:T(8,128)S(1)}, s32[1,8,8]{2,1,0:T(8,128)}, u32[]{:S(2)}) copy-start(s32[1,8,8]{2,1,0:T(8,128)} %param.14) | copy-start | bytes 772
  227.1 1.8 copy-start.3
  228.9 0.8 copy-start.4
  235.4 1.8 copy-start.3
  237.2 0.8 copy-start.4
  238.0 10.0 %copy-start.6 = (s32[8]{0:T(128)S(1)}, s32[8]{0:T(128)}, u32[]{:S(2)}) copy-start(s32[8]{0:T(128)} %get-tuple-element.508) | copy-start | bytes 100
Sparse Core Ops, SparseCore 0:
  9.1 63.9 all-gather.3
  74.9 60.6 all-gather.5
  137.5 61.0 all-gather.7
  291.4 171.0 reduce-scatter.1
where the time goes:
time: 471 us; the launch traced here: 469 us
  waiting for transfers between devices  295 us (63%)
  matrix products  71.4 us (15%)
  local copies, waits for them, and re-layouts  49 us (10%)
  loops' own time  29.6 us (6%)
  between operations  13.3 us (3%)
  other arithmetic  10.8 us (2%)
    reduce_scatter x1, waiting for transfers between devices, local(): lax.psum_scatter(head_terms.astype(jnp.bfloat16), 'mp', scatter_dimension...  171 us
    all_gather x1, waiting for transfers between devices, local(): lax.all_gather(kv_needed, 'dp', axis=1, tiled=True)  62.5 us
    all_gather x1, waiting for transfers between devices, local(): lax.all_gather(q_weight, 'dp', axis=1, tiled=True)  60.4 us
    dot_general x16, matrix products, project_one_block(): jnp.dot(row_block, lax.dynamic_index_in_dim(shard_piece, block_kind, 0, k...  40.6 us
    dot_general x8, matrix products, body_one_block(): return jnp.dot(row_block, chosen, preferred_element_type=jnp.float32)  23.2 us
    another operation x1, loops' own time, local(): partial_out = lax.map(body_one_block, (attended, block_kinds))  14.9 us
    dynamic_slice x16, local copies, waits for them, and re-layouts, project_rows(): products = lax.map(project_one_block, (blocks, block_kinds))  14.8 us
    another operation x1, loops' own time, project_rows(): products = lax.map(project_one_block, (blocks, block_kinds))  13.3 us
  transfers between devices with their start and end apart: 4, of which 3 were waited for; matrix products, arithmetic and copies ran while one was open for 19% of the time, Pallas kernels for 0%

commit v1 on v0

v1 whole, which is shorter than its diff:
```python
import functools

import jax
import jax.numpy as jnp
import numpy as np
from jax import lax
from jax.experimental import pallas as pl
from jax.experimental.pallas import tpu as pltpu
from jax.sharding import Mesh
from jax.sharding import PartitionSpec as P

D = 3584
HD = 128
BLK = 128
NBLK = 8
SEQ = 1024
ROWS = 112
NG = 32
NY = 4
QB = 4
HEADS = 4
WID = HEADS * HD
ROPE_THETA = 1000000.0
NEG = -1e30
ANY = pl.BlockSpec(memory_space=pl.ANY)
SM = pl.BlockSpec(memory_space=pltpu.SMEM)


def rotary_tables():
    half = HD // 2
    freq = ROPE_THETA ** (-np.arange(half, dtype=np.float64) * 2.0 / HD)
    ang = np.arange(SEQ, dtype=np.float64)[:, None] * freq[None, :]
    cos = np.concatenate([np.cos(ang), np.cos(ang)], axis=1)
    sin = np.concatenate([-np.sin(ang), np.sin(ang)], axis=1)
    return np.asarray(cos, np.float32), np.asarray(sin, np.float32)


def rotate(x, cos, sin):
    return x * cos + pltpu.roll(x, HD // 2, 1) * sin


def kv_body(mod, x_hbm, w_hbm, cos, sin, k_out, v_out, x, w, xsem, wsem):
    copies = []
    for m in range(2):
        c = pltpu.make_async_copy(w_hbm.at[:, m], w.at[m], wsem.at[m])
        c.start()
        copies.append(c)
    xc = []
    for b in range(NBLK):
        c = pltpu.make_async_copy(x_hbm.at[pl.ds(b * BLK, BLK)], x.at[b], xsem.at[b])
        c.start()
        xc.append(c)
    for c in copies:
        c.wait()
    for b in range(NBLK):
        xc[b].wait()
        y = jnp.dot(x[b], w[mod[b]].reshape(D, 2 * HD), preferred_element_type=jnp.float32)
        rows = pl.ds(b * BLK, BLK)
        k_out[rows, :] = rotate(y[:, :HD], cos[rows, :], sin[rows, :]).astype(jnp.bfloat16)
        v_out[rows, :] = y[:, HD:].astype(jnp.bfloat16)


def q_body(mod, pos, mask, x_hbm, w_hbm, cos, sin, k, v, att, x, w, q, s, xsem, wsem):
    zh = pos[1]
    copies = []
    for h in range(2):
        for g in range(4):
            for m in range(2):
                c = pltpu.make_async_copy(
                    w_hbm.at[g, h, :, m],
                    w.at[m, pl.ds(8 * g, 8), :, pl.ds(h * 2 * HD, 2 * HD)],
                    wsem.at[m],
                )
                c.start()
                copies.append(c)
    xc = []
    for i in range(QB):
        c = pltpu.make_async_copy(
            x_hbm.at[pl.ds((2 * i + zh) * BLK, BLK)], x.at[i], xsem.at[i]
        )
        c.start()
        xc.append(c)
    for c in copies:
        c.wait()
    for c in xc:
        c.wait()
    diff = lax.broadcasted_iota(jnp.int32, (BLK, BLK), 1) - lax.broadcasted_iota(
        jnp.int32, (BLK, BLK), 0
    )
    diff = jnp.concatenate([diff] * HEADS, axis=0)

    def one(i, carry):
        b = 2 * i + zh
        y = jnp.dot(x[i], w[mod[b]].reshape(D, WID), preferred_element_type=jnp.float32)
        rows = pl.ds(pl.multiple_of(b * BLK, BLK), BLK)
        ct, st = cos[rows, :], sin[rows, :]
        for h in range(HEADS):
            q[h * BLK : (h + 1) * BLK, :] = rotate(y[:, h * HD : (h + 1) * HD], ct, st).astype(
                jnp.bfloat16
            )
        qq = q[...]
        for j in range(NBLK):
            mb = mask[b, j]
            off = jnp.where(mb == 1, 4096, jnp.where(mb == 2, BLK * (b - j), -4096))
            sj = lax.dot_general(
                qq,
                k[j * BLK : (j + 1) * BLK, :],
                (((1,), (1,)), ((), ())),
                preferred_element_type=jnp.float32,
            )
            s[:, j * BLK : (j + 1) * BLK] = jnp.where(diff <= off, sj, NEG)
        sv = s[...]
        p = jnp.exp((sv - jnp.max(sv, axis=1, keepdims=True)) * (HD**-0.5))
        total = jnp.sum(p, axis=1, keepdims=True)
        a = jnp.dot(p.astype(jnp.bfloat16), v[...], preferred_element_type=jnp.float32) / total
        for h in range(HEADS):
            att[i, :, h * HD : (h + 1) * HD] = a[h * BLK : (h + 1) * BLK, :].astype(jnp.bfloat16)
        return carry

    lax.fori_loop(0, QB, one, 0)


def o_body(mod, pos, att, w_hbm, o0, o1, o2, o3, w, wsem):
    y0, zh = pos[0], pos[1]
    copies = []
    for h in range(2):
        for g in range(4):
            for m in range(2):
                c = pltpu.make_async_copy(
                    w_hbm.at[g, h, :, 2 + m],
                    w.at[m, pl.ds(8 * g, 8), :, pl.ds(h * 2 * HD, 2 * HD)],
                    wsem.at[m],
                )
                c.start()
                copies.append(c)
    for c in copies:
        c.wait()
    for s, out in ((2, o2), (1, o1), (3, o3), (0, o0)):
        i = lax.rem(y0 + s, NY)
        wm = w.at[mod[2 * i + zh]]
        a = att[i]
        for g in range(4):
            wt = wm[8 * g : 8 * g + 8].reshape(8 * ROWS, WID)
            r = lax.dot_general(a, wt, (((1,), (1,)), ((), ())), preferred_element_type=jnp.float32)
            out[:, g * 8 * ROWS : (g + 1) * 8 * ROWS] = r.astype(jnp.bfloat16)


VM = pl.BlockSpec(memory_space=pltpu.VMEM)
BF = jnp.bfloat16


def kv_call(mod, x, w, cos, sin):
    return pl.pallas_call(
        kv_body,
        out_shape=[jax.ShapeDtypeStruct((SEQ, HD), BF)] * 2,
        in_specs=[SM, ANY, ANY, VM, VM],
        out_specs=[VM, VM],
        scratch_shapes=[
            pltpu.VMEM((NBLK, BLK, D), BF),
            pltpu.VMEM((2, NG, ROWS, 2 * HD), BF),
            pltpu.SemaphoreType.DMA((NBLK,)),
            pltpu.SemaphoreType.DMA((2,)),
        ],
        cost_estimate=pl.CostEstimate(
            flops=2 * SEQ * D * 2 * HD, bytes_accessed=2 * SEQ * D + 8 * D * HD, transcendentals=0
        ),
    )(mod, x, w, cos, sin)


def q_call(mod, pos, mask, x, w, cos, sin, k, v):
    return pl.pallas_call(
        q_body,
        out_shape=jax.ShapeDtypeStruct((QB, BLK, WID), BF),
        in_specs=[SM, SM, SM, ANY, ANY, VM, VM, VM, VM],
        out_specs=VM,
        scratch_shapes=[
            pltpu.VMEM((QB, BLK, D), BF),
            pltpu.VMEM((2, NG, ROWS, WID), BF),
            pltpu.VMEM((HEADS * BLK, HD), BF),
            pltpu.VMEM((HEADS * BLK, SEQ), jnp.float32),
            pltpu.SemaphoreType.DMA((QB,)),
            pltpu.SemaphoreType.DMA((2,)),
        ],
        cost_estimate=pl.CostEstimate(
            flops=2 * QB * BLK * D * WID + 4 * QB * BLK * SEQ * WID,
            bytes_accessed=SEQ * D + 4 * D * WID,
            transcendentals=QB * BLK * HEADS * SEQ,
        ),
    )(mod, pos, mask, x, w, cos, sin, k, v)


def o_call(mod, pos, att, w):
    return pl.pallas_call(
        o_body,
        out_shape=[jax.ShapeDtypeStruct((BLK, D), BF)] * 4,
        in_specs=[SM, SM, VM, ANY],
        out_specs=[VM] * 4,
        scratch_shapes=[
            pltpu.VMEM((2, NG, ROWS, WID), BF),
            pltpu.SemaphoreType.DMA((2,)),
        ],
        cost_estimate=pl.CostEstimate(
            flops=2 * QB * BLK * D * WID, bytes_accessed=4 * D * WID, transcendentals=0
        ),
    )(mod, pos, att, w)


def local(tokens, modality, block_mask, q_weight, kv_weight, o_weight):
    y = lax.axis_index("y")
    zh = lax.axis_index("zh")
    pos = jnp.stack([y, zh]).astype(jnp.int32)
    mod = modality[0]
    mask = block_mask[0]
    x = tokens[0]
    cos, sin = (jnp.asarray(t) for t in rotary_tables())
    kv = lax.dynamic_slice_in_dim(kv_weight, y * (2 * HD), 2 * HD, 2)
    qo = jnp.concatenate([q_weight, jnp.swapaxes(o_weight, 1, 2)], axis=0)
    kv_all = lax.all_gather(kv, ("x", "zl", "c"), axis=0)
    qo_all = lax.all_gather(qo, ("x", "zh", "zl", "c"), axis=0)
    qo_all = qo_all.reshape(4, 2, 8, 4, ROWS, 2 * HD)
    k, v = kv_call(mod, x, kv_all, cos, sin)
    att = q_call(mod, pos, mask, x, qo_all, cos, sin, k, v)
    outs = o_call(mod, pos, att, qo_all)
    total = outs[0].astype(jnp.float32)
    for s in (2, 1, 3):
        got = lax.ppermute(outs[s], "y", [(i, (i + s) % NY) for i in range(NY)])
        total = total + got.astype(jnp.float32)
    return total.astype(BF)[None]


def solution(mesh):
    fine = Mesh(mesh.devices.reshape(4, 4, 2, 4, 2), ("x", "zl", "c", "y", "zh"))
    dp = ("x", "zl", "c")
    mp = ("y", "zh")
    in_specs = (
        P(dp, None, None),
        P(dp, None),
        P(dp, None, None),
        P(None, dp, mp),
        P(None, dp, None),
        P(None, mp, dp),
    )
    return jax.shard_map(
        local, mesh=fine, in_specs=in_specs, out_specs=P(dp, mp, None), check_vma=False
    )
```

time: 471 us -> 248 us (0.53)
  waiting for transfers between devices: 295 us -> 184 us
  matrix products: 71.4 us -> 0 us
  local copies, waits for them, and re-layouts: 49 us -> 1.68 us
  Pallas kernels: 0 us -> 35.2 us
  loops' own time: 29.6 us -> 0 us
  starting transfers between devices: 0.13 us -> 6.39 us
  other arithmetic: 10.8 us -> 4.95 us
    reduce_scatter x1 -> x0, waiting for transfers between devices: 171 us -> none  [local(): lax.psum_scatter(head_terms.astype(jnp.bfloat16), 'mp', scatter_dimension...]
    dot_general x28 -> x0, matrix products: 71.4 us -> none  [the longest x16 40.6 us: project_one_block(): jnp.dot(row_block, lax.dynamic_index_in_dim(shard_piece, block_kind, 0, k...]
    ppermute x0 -> x3, waiting for transfers between devices: none -> 37.7 us  [local(): got = lax.ppermute(outs[s], 'y', [(i, (i + s) % NY) for i in range(NY)])]
    pallas_call x0 -> x3, Pallas kernels: none -> 35.2 us  [the longest x1 14 us: q_call(): pl.pallas_call(q_body, out_shape=jax.ShapeDtypeStruct((QB, BLK, WID), BF)...]
    another operation x3 -> x0, loops' own time: 29.6 us -> none  [the longest x1 14.9 us: local(): partial_out = lax.map(body_one_block, (attended, block_kinds))]
    all_gather x3 -> x2, waiting for transfers between devices: 123 us -> 147 us  [the longest x1 84 us: local(): qo_all = lax.all_gather(qo, ('x', 'zh', 'zl', 'c'), axis=0)]
    dynamic_slice x19 -> x1, local copies, waits for them, and re-layouts: 16.5 us -> 0.66 us  [local(): kv = lax.dynamic_slice_in_dim(kv_weight, y * (2 * HD), 2 * HD, 2)]
    while x9 -> x0, local copies, waits for them, and re-layouts: 11.6 us -> none  [the longest x1 10 us: local(): partial_out = lax.map(body_one_block, (attended, block_kinds))]
  transfers between devices with their start and end apart: 4 -> 5, of which waited for: 3 -> 5; matrix products, arithmetic and copies ran while one was open for 19% -> 1% of each run, Pallas kernels for 0% -> 5%
where the time goes in v1:
time: 248 us; the launch traced here: 246 us
  waiting for transfers between devices  184 us (74%)
  Pallas kernels  35.2 us (14%)
  between operations  13.4 us (5%)
  starting transfers between devices  6.39 us (3%)
  other arithmetic  4.95 us (2%)
    all_gather x1, waiting for transfers between devices, local(): qo_all = lax.all_gather(qo, ('x', 'zh', 'zl', 'c'), axis=0)  84 us
    all_gather x1, waiting for transfers between devices, local(): kv_all = lax.all_gather(kv, ('x', 'zl', 'c'), axis=0)  62.6 us
    ppermute x3, waiting for transfers between devices, local(): got = lax.ppermute(outs[s], 'y', [(i, (i + s) % NY) for i in range(NY)])  37.7 us
    pallas_call x1, Pallas kernels, q_call(): pl.pallas_call(q_body, out_shape=jax.ShapeDtypeStruct((QB, BLK, WID), BF)...  14 us
    pallas_call x1, Pallas kernels, kv_call(): pl.pallas_call(kv_body, out_shape=[jax.ShapeDtypeStruct((SEQ, HD), BF)] *...  11.5 us
    pallas_call x1, Pallas kernels, o_call(): pl.pallas_call(o_body, out_shape=[jax.ShapeDtypeStruct((BLK, D), BF)] * 4...  9.69 us
    ppermute x3, starting transfers between devices, local(): got = lax.ppermute(outs[s], 'y', [(i, (i + s) % NY) for i in range(NY)])  6.34 us
  transfers between devices with their start and end apart: 5, of which 5 were waited for; matrix products, arithmetic and copies ran while one was open for 1% of the time, Pallas kernels for 5%

profile of v1, /device:TPU:32, one launch (start us, length us, event | category | flops | bytes accessed | tf_op | source)
XLA Modules:
  0.0 246.0 jit_solution(6312596300740250698)
XLA Ops:
  6.5 0.0 copy-start
  6.5 0.0 all-gather.7.cloned.1.call-start
  6.5 1.0 copy-done
  7.6 0.7 constant_dynamic-slice_fusion
  8.2 0.0 all-gather.7.cloned.1.call-update
  8.2 0.0 all-gather.5.cloned.1.call-start
  8.3 1.7 pad_maximum_fusion
  10.0 0.0 all-gather.5.cloned.1.call-update
  10.0 0.7 pad_add_fusion.pos
  10.6 62.6 %all-gather.7.cloned.1.call-done = bf16[64,112,256]{2,1,0:T(8,128)(2,1)} async-done(((bf16[2,112,256]{2,1,0:T(8,128)(2,1)}), bf16[64,112,256]{2,1,0:T(8,128)(2,1)}) %all-gather.7.cloned.1.call-update) | async-done | bytes 3670032 | tf_op jit(solution)/shard_map/all_gather | solution.py:218
  73.2 11.5 %shard_map.82 = (bf16[1024,128]{1,0:T(8,128)(2,1)}, bf16[1024,128]{1,0:T(8,128)(2,1)}) custom-call(s32[8]{0:T(128)} %bitcast.16, bf16[1024,3584]{1,0:T(8,128)(2,1)} %bitcast.12, bf16[32,2,112,256]{3,2,1,0:T(8,128)(2,1)} %bitcast.14, f32[1024,128]{1,0:T(8,128)} %constant.18.clone.cos, f32[1024,128]{1,0:T(8,128)} %constant.19.clone.sin), custom_call_target="tpu_custom_call" | custom-call | flops 1879048192 | bytes 11010048 | tf_op jit(solution)/shard_map/pallas_call | solution.py:153
  84.7 84.0 %all-gather.5.cloned.1.call-done = bf16[256,112,256]{2,1,0:T(8,128)(2,1)} async-done(((bf16[4,112,256]{2,1,0:T(8,128)(2,1)}), bf16[256,112,256]{2,1,0:T(8,128)(2,1)}) %all-gather.5.cloned.1.call-update) | async-done | bytes 14680080 | tf_op jit(solution)/shard_map/all_gather | solution.py:219
  168.7 14.0 %shard_map.83.att = bf16[4,128,512]{2,1,0:T(8,128)(2,1)} custom-call(s32[8]{0:T(128)} %bitcast.17, s32[2]{0:T(128)} %pad_add_fusion.pos, s32[8,8]{1,0:T(8,128)} %bitcast.19, bf16[1024,3584]{1,0:T(8,128)(2,1)} %bitcast.13, bf16[4,2,8,4,112,256]{5,4,3,2,1,0:T(8,128)(2,1)} %bitcast.10, f32[1024,128]{1,0:T(8,128)} %constant.18.clone.cos, ...), custom_call_target="tpu_custom_call" | custom-call | flops 2952790016 | bytes 11010048 | tf_op jit(solution)/shard_map/pallas_call | solution.py:171
  182.7 9.7 %shard_map.84 = (bf16[128,3584]{1,0:T(8,128)(2,1)}, bf16[128,3584]{1,0:T(8,128)(2,1)}, bf16[128,3584]{1,0:T(8,128)(2,1)}, bf16[128,3584]{1,0:T(8,128)(2,1)}) custom-call(s32[8]{0:T(128)} %bitcast.18, s32[2]{0:T(128)} %pad_add_fusion.pos, bf16[4,128,512]{2,1,0:T(8,128)(2,1)} %shard_map.83.att, bf16[4,2,8,4,112,256]{5,4,3,2,1,0:T(8,128)(2,1)} %bitcast.11), custom_call_target="tpu_custom_call" | custom-call | flops 1879048192 | bytes 7340032 | tf_op jit(solution)/shard_map/pallas_call | solution.py:193
  192.4 3.1 %collective-permute-start = (bf16[128,3584]{1,0:T(8,128)(2,1)}, bf16[128,3584]{1,0:T(8,128)(2,1)S(1)}, u32[]{:S(2)}, u32[]{:S(2)}) collective-permute-start(bf16[128,3584]{1,0:T(8,128)(2,1)} %get-tuple-element.14), channel_id=1, source_target_pairs={{0,4},{2,6},{4,0},{6,2},{1,5},{3,7},{5,1},{7,3},{8,12},{10,14},{12... | collective-permute-start | bytes 2752520 | tf_op jit(solution)/shard_map/ppermute | solution.py:226
  195.5 0.6 collective-permute-start.1
  196.1 2.7 %collective-permute-start.2 = (bf16[128,3584]{1,0:T(8,128)(2,1)}, bf16[128,3584]{1,0:T(8,128)(2,1)S(1)}, u32[]{:S(2)}, u32[]{:S(2)}) collective-permute-start(bf16[128,3584]{1,0:T(8,128)(2,1)} %get-tuple-element.16), channel_id=1, source_target_pairs={{0,6},{2,0},{4,2},{6,4},{1,7},{3,1},{5,3},{7,5},{8,14},{10,8},{12,... | collective-permute-start | bytes 2752520 | tf_op jit(solution)/shard_map/ppermute | solution.py:226
  198.8 18.7 %collective-permute-done = bf16[128,3584]{1,0:T(8,128)(2,1)S(1)} collective-permute-done((bf16[128,3584]{1,0:T(8,128)(2,1)}, bf16[128,3584]{1,0:T(8,128)(2,1)S(1)}, u32[]{:S(2)}, u32[]{:S(2)}) %collective-permute-start) | collective-permute-done | bytes 917536 | tf_op jit(solution)/shard_map/ppermute | solution.py:226
  217.5 18.9 %collective-permute-done.1 = bf16[128,3584]{1,0:T(8,128)(2,1)S(1)} collective-permute-done((bf16[128,3584]{1,0:T(8,128)(2,1)}, bf16[128,3584]{1,0:T(8,128)(2,1)S(1)}, u32[]{:S(2)}, u32[]{:S(2)}) %collective-permute-start.1) | collective-permute-done | bytes 917536 | tf_op jit(solution)/shard_map/ppermute | solution.py:226
  236.4 0.1 collective-permute-done.2
  236.5 2.6 %fusion = bf16[1,128,3584]{2,1,0:T(8,128)(2,1)} fusion(bf16[128,3584]{1,0:T(8,128)(2,1)S(1)} %collective-permute-done.2, bf16[128,3584]{1,0:T(8,128)(2,1)S(1)} %collective-permute-done.1, bf16[128,3584]{1,0:T(8,128)(2,1)S(1)} %collective-permute-done, bf16[128,3584]{1,0:T(8,128)(2,1)} %get-tuple-element.13), kind=kLoop, calls=%fused_computation.1 | loop fusion | flops 3670016 | bytes 4587520 | tf_op jit(solution)/shard_map/broadcast_in_dim | solution.py:228
Async XLA Ops:
  6.5 1.0 copy-start
  6.5 66.7 %all-gather.7.cloned.1.call-start = ((), (), s32[]{:S(2)}) async-start(), calls=%async_computation.1 | async-start | bytes 3784704 | tf_op jit(solution)/shard_map/all_gather | solution.py:218
  8.2 160.5 %all-gather.5.cloned.1.call-start = ((), (), s32[]{:S(2)}) async-start(), calls=%async_computation | async-start | bytes 14909440 | tf_op jit(solution)/shard_map/all_gather | solution.py:219
  192.4 25.1 %collective-permute-start = (bf16[128,3584]{1,0:T(8,128)(2,1)}, bf16[128,3584]{1,0:T(8,128)(2,1)S(1)}, u32[]{:S(2)}, u32[]{:S(2)}) collective-permute-start(bf16[128,3584]{1,0:T(8,128)(2,1)} %get-tuple-element.14), channel_id=1, source_target_pairs={{0,4},{2,6},{4,0},{6,2},{1,5},{3,7},{5,1},{7,3},{8,12},{10,14},{12... | collective-permute-start | bytes 2752520 | tf_op jit(solution)/shard_map/ppermute | solution.py:226
  195.5 40.9 %collective-permute-start.1 = (bf16[128,3584]{1,0:T(8,128)(2,1)}, bf16[128,3584]{1,0:T(8,128)(2,1)S(1)}, u32[]{:S(2)}, u32[]{:S(2)}) collective-permute-start(bf16[128,3584]{1,0:T(8,128)(2,1)} %get-tuple-element.15), channel_id=1, source_target_pairs={{0,2},{2,4},{4,6},{6,0},{1,3},{3,5},{5,7},{7,1},{8,10},{10,12},{12... | collective-permute-start | bytes 2752520 | tf_op jit(solution)/shard_map/ppermute | solution.py:226
  196.1 40.4 %collective-permute-start.2 = (bf16[128,3584]{1,0:T(8,128)(2,1)}, bf16[128,3584]{1,0:T(8,128)(2,1)S(1)}, u32[]{:S(2)}, u32[]{:S(2)}) collective-permute-start(bf16[128,3584]{1,0:T(8,128)(2,1)} %get-tuple-element.16), channel_id=1, source_target_pairs={{0,6},{2,0},{4,2},{6,4},{1,7},{3,1},{5,3},{7,5},{8,14},{10,8},{12,... | collective-permute-start | bytes 2752520 | tf_op jit(solution)/shard_map/ppermute | solution.py:226
Sparse Core Ops, SparseCore 0:
  9.2 63.9 all-gather.6
  75.9 92.7 all-gather.4
